TPU v7x, 256 devices: a whole 4x4x8 slice. The times are simulated.
256 devices in a mesh: half: 2 (over core), prow: 16 (over z, x_hi), pcol: 8 (over x_lo, y).
Axes of the slice: x: 4 (x_hi: 2, x_lo: 2; x = x_hi * 2 + x_lo), y: 4, z: 8, core: 2. Of those that a mesh axis runs over, the one named last changes fastest.
Arguments:
- child_update: float32 [2, 8192, 8192], P('half', 'prow', 'pcol'), may hold values from -6 to 6, as said below
- child_panel: float32 [2, 8192, 1024], P('half', 'prow'), may hold values from -3 to 3
- root_front: float32 [12288, 12288], P('prow', ('half', 'pcol')), may hold values from -29 to 6144, as said below
- index_map: int32 [2, 64], replicated, may hold values from 0 to 95, as said below
Outputs:
- root_next: float32 [12288, 12288], P('prow', ('half', 'pcol'))
Inputs may be any that keep to these rules, and one draw needn't show every extreme that they name: `child_update`: each child's matrix is symmetric. `root_front`: Symmetric. `index_map`: for each child the entries are distinct, and child 0 names the blocks 0 to 1. Of the 8 blocks of one process row of both children (blocks p * 4 on), at most 1 share one root process row v // 6; of the 8 blocks of one child process column (blocks q * 8 on), at most 1 share one root column group v // 6; both bounds are reached.
All inputs are finite; a program needn't handle non-finite values.
Results may differ from a plain program's by a relative error of at most 0.00016.
Values sent between devices are 32-bit elements; how exact they have to be, the bound alone decides.
A program may use at most 128 MiB of HBM per device.

v0:
```python
import jax
import jax.numpy as jnp
from jax import lax
from jax.sharding import PartitionSpec as P

BLK = 128
RP = 256


def spread_2(value, axis, source):
    kept = jnp.where(lax.axis_index(axis) == source, value, 0).astype(value.dtype)
    return lax.psum(kept, axis)


def ranking(labels, count):
    onehot = (labels[..., None] == jnp.arange(count, dtype=jnp.int32)).astype(jnp.int32)
    return jnp.sum((jnp.cumsum(onehot, axis=-2) - 1) * onehot, axis=-1)


def solve_rows(factor, raw_rows, global_rows):
    solved = lax.linalg.triangular_solve(
        factor, raw_rows, left_side=False, lower=True, transpose_a=True
    )
    leading = jnp.concatenate(
        [factor, jnp.zeros((raw_rows.shape[0] - RP, RP), jnp.float32)], axis=0
    )
    return jnp.where(global_rows[:, None] < RP, leading, solved)


def shards(child_update, child_panel, root_front, index_map):
    highest = lax.Precision.HIGHEST
    rows_dev = child_update.shape[1]
    cols_dev = child_update.shape[2]
    col_count = lax.axis_size("pcol")
    row_count = lax.axis_size("prow")
    row_ratio = row_count // col_count
    group_count = 2 * col_count
    column_index = lax.axis_index("pcol")
    child_index = lax.axis_index("half")
    row_index = lax.axis_index("prow")
    group_index = lax.axis_index(("half", "pcol"))
    own_panel = child_panel[0]
    pieces = []
    for offset in range(row_ratio):
        remote = spread_2(own_panel, "prow", column_index * row_ratio + offset)
        product = lax.dot_general(
            own_panel,
            remote,
            (((1,), (1,)), ((), ())),
            precision=highest,
            preferred_element_type=jnp.float32,
        )
        pieces.append(child_update[0, :, offset * rows_dev : (offset + 1) * rows_dev] - product)
    schur_part = jnp.concatenate(pieces, axis=1)
    root_rows = root_front.shape[0]
    root_cols = root_front.shape[1]
    child_blocks = rows_dev // BLK
    col_blocks = cols_dev // BLK
    row_blocks = root_rows // BLK
    group_cols = root_cols // BLK
    cap_col = max(1, col_blocks // group_count)
    cap_row = max(1, 2 * child_blocks // row_count)
    by_column = index_map.reshape(2, col_count, col_blocks)
    by_row = index_map.reshape(2, row_count, child_blocks)
    col_groups = by_column // group_cols
    col_ranks = ranking(col_groups, group_count)
    row_owners = by_row // row_blocks
    arrives = col_groups == group_index
    col_slots = by_column - group_index * group_cols
    col_place = (
        arrives[:, :, :, None, None]
        & (col_ranks[:, :, :, None, None] == jnp.arange(cap_col, dtype=jnp.int32)[:, None])
        & (col_slots[:, :, :, None, None] == jnp.arange(group_cols, dtype=jnp.int32))
    ).astype(jnp.float32)
    col_place = jnp.sum(col_place, axis=2)
    row_local = by_row - row_index * row_blocks
    local_onehot = (row_local[..., None] == jnp.arange(row_blocks, dtype=jnp.int32)).astype(
        jnp.float32
    )
    own_groups = col_groups[child_index, column_index]
    own_col_ranks = col_ranks[child_index, column_index]
    col_select = (
        (own_groups[None, None, :] == jnp.arange(group_count, dtype=jnp.int32)[:, None, None])
        & (own_col_ranks[None, None, :] == jnp.arange(cap_col, dtype=jnp.int32)[None, :, None])
    ).astype(jnp.float32)
    child_ranks = ranking(row_owners, row_count)
    own_owner = row_owners[child_index, row_index]
    own_rank = child_ranks[child_index, row_index]
    row_select = (
        (own_owner[None, None, :] == jnp.arange(row_count, dtype=jnp.int32)[:, None, None])
        & (own_rank[None, None, :] == jnp.arange(cap_row, dtype=jnp.int32)[None, :, None])
    ).astype(jnp.float32)
    outgoing_rows = jnp.einsum(
        "tri,iyk->tryk",
        row_select,
        schur_part.reshape(child_blocks, BLK, cols_dev),
        precision=highest,
    )
    arrived = lax.all_to_all(outgoing_rows, "prow", split_axis=0, concat_axis=0, tiled=True)
    arrived_tiles = arrived.reshape(row_count, cap_row, BLK, col_blocks, BLK)
    outgoing = jnp.einsum("guj,pryjk->gupryk", col_select, arrived_tiles, precision=highest)
    incoming = lax.all_to_all(outgoing, ("half", "pcol"), split_axis=0, concat_axis=0, tiled=True)
    incoming = incoming.reshape(2, col_count, cap_col, row_count, cap_row, BLK, BLK)
    slot_item = (
        (row_owners[:, :, None, :] == row_index)
        & (child_ranks[:, :, None, :] == jnp.arange(cap_row, dtype=jnp.int32)[None, None, :, None])
    ).astype(jnp.float32)
    row_place = jnp.einsum("cpri,cpiw->cprw", slot_item, local_onehot, precision=highest)
    spread = jnp.einsum("cqus,cqupryz->cprysz", col_place, incoming, precision=highest)
    extended = jnp.einsum("cprw,cprysz->wysz", row_place, spread, precision=highest)
    assembled = root_front + extended.reshape(root_rows, root_cols)
    global_rows = row_index * root_rows + jnp.arange(root_rows, dtype=jnp.int32)
    global_cols = group_index * root_cols + jnp.arange(root_cols, dtype=jnp.int32)
    group_ratio = row_count // group_count
    raw_panel = assembled[:, :RP]
    pivot_block = spread_2(assembled[:RP, :RP], "prow", 0)
    factor = jnp.linalg.cholesky(pivot_block)
    own_rows = solve_rows(factor, raw_panel, global_rows)
    row_panel = spread_2(own_rows, ("half", "pcol"), 0)
    offset = 0
    across = spread_2(row_panel, "prow", group_index * group_ratio + offset)
    update = lax.dot_general(
        row_panel,
        across,
        (((1,), (1,)), ((), ())),
        precision=highest,
        preferred_element_type=jnp.float32,
    )
    trailing_mask = (global_rows[:, None] >= RP) & (global_cols[None, :] >= RP)
    trailing = assembled - jnp.where(trailing_mask, update, 0.0)
    first_group = group_index == 0
    panel_cols = jnp.where(first_group, row_panel, trailing[:, :RP])
    return jnp.concatenate([panel_cols, trailing[:, RP:]], axis=1)


def solution(mesh):
    return jax.shard_map(
        shards,
        mesh=mesh,
        in_specs=(
            P("half", "prow", "pcol"),
            P("half", "prow", None),
            P("prow", ("half", "pcol")),
            P(),
        ),
        out_specs=P("prow", ("half", "pcol")),
        check_vma=False,
    )
```

profile of v0, /device:TPU:8, one launch (start us, length us, event | category | flops | bytes accessed | tf_op | source)
XLA Modules:
  0.0 1266.6 jit_solution(17898139743299591110)
XLA Ops:
  6.5 4.3 bitcast_select_fusion.1
  10.9 1.6 copy-done.4
  15.0 1.6 copy.122
  17.7 205.5 %all-reduce.14.cloned.1.call-done = (f32[512,1024]{1,0:T(8,128)}, f32[512,1024]{1,0:T(8,128)}) async-done(((f32[512,1024]{1,0:T(8,128)}, f32[512,1024]{1,0:T(8,128)}), (f32[512,1024]{1,0:T(8,128)}, f32[512,1024]{1,0:T(8,128)})) %all-reduce.14.cloned.1.call-update) | async-done | bytes 4194320 | tf_op jit(solution)/shard_map/psum | solution.py:12
  223.2 5.6 fusion.18
  228.8 3.6 fusion.24
  232.6 2.0 reshape.343
  234.6 3.0 copy.92
  237.6 4.1 convolution_bitcast_fusion.1
  241.6 8.1 copy.93
  249.7 6.4 all-to-all-start
  256.9 188.2 %all-to-all-done = f32[16,1,128,1024]{3,2,1,0:T(8,128)} async-done(((f32[16,1,128,1024]{3,2,1,0:T(8,128)}), f32[16,1,128,1024]{3,2,1,0:T(8,128)}, u32[]{:S(2)}, u32[]{:S(2)}) %all-to-all-start) | async-done | bytes 8388640 | tf_op jit(solution)/shard_map/all_to_all | solution.py:99
  445.0 5.5 copy.125
  450.5 8.2 convolution_bitcast_fusion
  458.7 10.7 copy.94
  469.4 5.2 all-to-all-start.1
  474.9 2.0 copy.98
  477.2 197.5 %all-to-all-done.1 = f32[16,1,16,1,128,128]{5,4,2,3,1,0:T(8,128)} async-done(((f32[16,1,16,1,128,128]{5,4,2,3,1,0:T(8,128)}), f32[16,1,16,1,128,128]{5,4,2,3,1,0:T(8,128)}, u32[]{:S(2)}, u32[]{:S(2)}) %all-to-all-start.1) | async-done | bytes 16777248 | tf_op jit(solution)/shard_map/all_to_all | solution.py:102
  674.7 32.3 %fusion.5 = f32[2,16,128,6,128]{4,3,2,1,0:T(8,128)} fusion(f32[2,8,16,128,128]{4,3,2,1,0:T(8,128)} %bitcast.15, f32[2,8,6]{1,2,0:T(8,128)S(1)} %convert_reduce_fusion), kind=kOutput, calls=%fused_computation.8 | convolution fusion | flops 301989888 | bytes 29360512 | tf_op jit(solution)/shard_map/cqus,cqupryz->cprysz/dot_general | solution.py:109
  707.0 17.1 %fusion.12 = f32[6,128,6,128]{3,0,2,1:T(8,128)S(1)} fusion(f32[2,16,128,6,128]{4,3,2,1,0:T(8,128)} %fusion.5, f32[2,16,6]{2,1,0:T(8,128)S(1)} %select_reduce_fusion), kind=kOutput, calls=%fused_computation.20 | convolution fusion | flops 226492416 | bytes 14942976 | tf_op jit(solution)/shard_map/cprw,cprysz->wysz/dot_general | solution.py:110
  724.0 2.4 copy.118
  726.4 3.3 bitcast_add_fusion
  730.6 158.1 %all-reduce.8.cloned.1.call-done = f32[256,256]{0,1:T(8,128)} async-done(((f32[256,256]{0,1:T(8,128)}), f32[256,256]{0,1:T(8,128)}) %all-reduce.8.cloned.1.call-update) | async-done | bytes 262160 | tf_op jit(solution)/shard_map/psum | solution.py:12
  890.7 11.7 cholesky.49
  902.5 9.8 custom-call.14
  912.8 11.7 cholesky.103
  927.1 4.5 while.1
  931.6 19.7 %custom-call.15 = f32[2,128,128]{1,2,0:T(8,128)S(1)} custom-call(f32[2,128,128]{2,1,0:T(8,128)S(1)} %get-tuple-element.12), custom_call_target="InvertDiagBlocksLowerTriangular" | custom-call | tf_op jit(solution)/shard_map/triangular_solve | solution.py:21
  953.9 135.7 %all-reduce.10.cloned.1.call-done = f32[768,256]{0,1:T(8,128)} async-done(((f32[768,256]{0,1:T(8,128)}), f32[768,256]{0,1:T(8,128)}) %all-reduce.10.cloned.1.call-update) | async-done | bytes 786448 | tf_op jit(solution)/shard_map/psum | solution.py:12
  1090.6 163.4 %all-reduce.12.cloned.1.call-done = f32[768,256]{0,1:T(8,128)} async-done(((f32[768,256]{0,1:T(8,128)}), f32[768,256]{0,1:T(8,128)}) %all-reduce.12.cloned.1.call-update) | async-done | bytes 786448 | tf_op jit(solution)/shard_map/psum | solution.py:12
  1254.0 3.6 select_subtract_fusion
  1257.9 2.0 copy.106
  (87 shorter events, 17.9 us)
Async XLA Ops:
  6.5 216.7 %all-reduce.14.cloned.1.call-start = ((), (), s32[]{:S(2)}) async-start(), calls=%async_computation.5 | async-start | bytes 8388608 | tf_op jit(solution)/shard_map/psum | solution.py:12
  10.9 1.6 copy-start.4
  13.6 2.9 copy-start.5
  13.6 209.6 %copy-start = (f32[1,512,1024]{2,1,0:T(8,128)S(1)}, f32[1,512,1024]{2,1,0:T(8,128)}, u32[]{:S(2)}) copy-start(f32[1,512,1024]{2,1,0:T(8,128)} %param.5) | copy-start | bytes 6291460
  223.2 5.6 copy-start.3
  249.7 195.3 %all-to-all-start = ((f32[16,1,128,1024]{3,2,1,0:T(8,128)}), f32[16,1,128,1024]{3,2,1,0:T(8,128)}, u32[]{:S(2)}, u32[]{:S(2)}) async-start(f32[16,1,128,1024]{3,2,1,0:T(8,128)} %copy.93), calls=%async_computation | async-start | bytes 16777216 | tf_op jit(solution)/shard_map/all_to_all | solution.py:99
  469.4 5.6 copy-start.2
  469.4 205.3 %all-to-all-start.1 = ((f32[16,1,16,1,128,128]{5,4,2,3,1,0:T(8,128)}), f32[16,1,16,1,128,128]{5,4,2,3,1,0:T(8,128)}, u32[]{:S(2)}, u32[]{:S(2)}) async-start(f32[16,1,16,1,128,128]{5,4,2,3,1,0:T(8,128)} %copy.94), calls=%async_computation.1 | async-start | bytes 33554432 | tf_op jit(solution)/shard_map/all_to_all | solution.py:102
  474.6 414.0 %all-reduce.8.cloned.1.call-start = ((), (), s32[]{:S(2)}) async-start(), calls=%async_computation.2 | async-start | bytes 524288 | tf_op jit(solution)/shard_map/psum | solution.py:12
  730.5 359.1 %all-reduce.10.cloned.1.call-start = ((), (), s32[]{:S(2)}) async-start(), calls=%async_computation.3 | async-start | bytes 1572864 | tf_op jit(solution)/shard_map/psum | solution.py:12
  953.8 300.1 %all-reduce.12.cloned.1.call-start = ((), (), s32[]{:S(2)}) async-start(), calls=%async_computation.4 | async-start | bytes 1572864 | tf_op jit(solution)/shard_map/psum | solution.py:12
  1089.6 164.4 %copy-start.1 = (f32[768,256]{0,1:T(8,128)S(1)}, f32[768,256]{0,1:T(8,128)}, u32[]{:S(2)}) copy-start(f32[768,256]{0,1:T(8,128)} %all-reduce.10.cloned.1.call-done) | copy-start | bytes 2359300
Sparse Core Ops, SparseCore 0:
  11.0 212.1 all-reduce.13
  730.6 157.9 all-reduce.7
  953.9 135.5 all-reduce.9
  1092.1 161.8 all-reduce.11
where the time goes:
time: 1270 us
  waiting for transfers between devices  1050 us (83%)
  matrix products  76.4 us (6%)
  other arithmetic  66.8 us (5%)
  local copies, waits for them, and re-layouts  47.9 us (4%)
  between operations  15.1 us (1%)
    psum x4, waiting for transfers between devices, spread_2(): return lax.psum(kept, axis)  663 us
    all_to_all x1, waiting for transfers between devices, shards(): lax.all_to_all(outgoing, ('half', 'pcol'), split_axis=0, concat_axis=0, t...  198 us
    all_to_all x1, waiting for transfers between devices, shards(): lax.all_to_all(outgoing_rows, 'prow', split_axis=0, concat_axis=0, tiled=...  188 us
    another operation x6, other arithmetic, shards(): factor = jnp.linalg.cholesky(pivot_block)  34 us
    dot_general x1, matrix products, shards(): jnp.einsum('cqus,cqupryz->cprysz', col_place, incoming, precision=highest)  32.3 us
  transfers between devices with their start and end apart: 6, of which 6 were waited for; matrix products, arithmetic and copies ran while one was open for 1% of the time, Pallas kernels for 0%

commit v1 on v0

--- a/solution.py
+++ b/solution.py
@@ -9,7 +9,7 @@
 
 def spread_2(value, axis, source):
     kept = jnp.where(lax.axis_index(axis) == source, value, 0).astype(value.dtype)
-    return lax.psum(kept, axis)
+    return jnp.sum(lax.all_gather(kept, axis), axis=0)
 
 
 def ranking(labels, count):

time: 1270 us -> 1810 us (1.43)
  waiting for transfers between devices: 1050 us -> 1550 us
  other arithmetic: 66.8 us -> 108 us
    all_gather x0 -> x5, waiting for transfers between devices: none -> 1150 us  [spread_2(): return jnp.sum(lax.all_gather(kept, axis), axis=0)]
    psum x4 -> x0, waiting for transfers between devices: 663 us -> none  [spread_2(): return lax.psum(kept, axis)]
    reduce_sum x0 -> x5, other arithmetic: none -> 41.3 us  [spread_2(): return jnp.sum(lax.all_gather(kept, axis), axis=0)]
  transfers between devices with their start and end apart: 6 -> 7, of which waited for: 6 -> 7; matrix products, arithmetic and copies ran while one was open for 1% -> 1% of each run, Pallas kernels for 0% -> 0%
where the time goes in v1:
time: 1810 us; the launch traced here: 1800 us
  waiting for transfers between devices  1550 us (86%)
  other arithmetic  108 us (6%)
  matrix products  79.3 us (4%)
  local copies, waits for them, and re-layouts  40.8 us (2%)
    all_gather x5, waiting for transfers between devices, spread_2(): return jnp.sum(lax.all_gather(kept, axis), axis=0)  1150 us
    all_to_all x1, waiting for transfers between devices, shards(): lax.all_to_all(outgoing, ('half', 'pcol'), split_axis=0, concat_axis=0, t...  201 us
    all_to_all x1, waiting for transfers between devices, shards(): lax.all_to_all(outgoing_rows, 'prow', split_axis=0, concat_axis=0, tiled=...  191 us
    reduce_sum x5, other arithmetic, spread_2(): return jnp.sum(lax.all_gather(kept, axis), axis=0)  41.3 us
  transfers between devices with their start and end apart: 7, of which 7 were waited for; matrix products, arithmetic and copies ran while one was open for 1% of the time, Pallas kernels for 0%

profile of v1, /device:TPU:8, one launch (start us, length us, event | category | flops | bytes accessed | tf_op | source)
XLA Modules:
  0.0 1801.5 jit_solution(7543689544211507227)
XLA Ops:
  6.5 4.3 broadcast_select_fusion.1
  16.2 410.3 %all-gather.9.cloned.1.call-done = f32[16,512,1024]{2,1,0:T(8,128)} async-done(((f32[1,512,1024]{2,1,0:T(8,128)}), f32[16,512,1024]{2,1,0:T(8,128)}) %all-gather.9.cloned.1.call-update) | async-done | bytes 33554448 | tf_op jit(solution)/shard_map/all_gather | solution.py:12
  426.5 13.6 reduce_sum.74
  440.0 6.7 fusion.18
  446.7 391.7 %all-gather.11.cloned.1.call-done = f32[16,512,1024]{2,1,0:T(8,128)} async-done(((f32[1,512,1024]{2,1,0:T(8,128)}), f32[16,512,1024]{2,1,0:T(8,128)}) %all-gather.11.cloned.1.call-update) | async-done | bytes 33554448 | tf_op jit(solution)/shard_map/all_gather | solution.py:12
  838.5 13.4 reduce_sum.75
  851.9 5.2 fusion.24
  859.0 3.4 copy.70
  862.5 4.1 convolution_bitcast_fusion.1
  866.6 8.1 copy.71
  874.6 4.9 all-to-all-start
  880.3 191.4 %all-to-all-done = f32[16,1,128,1024]{3,2,1,0:T(8,128)} async-done(((f32[16,1,128,1024]{3,2,1,0:T(8,128)}), f32[16,1,128,1024]{3,2,1,0:T(8,128)}, u32[]{:S(2)}, u32[]{:S(2)}) %all-to-all-start) | async-done | bytes 8388640 | tf_op jit(solution)/shard_map/all_to_all | solution.py:99
  1071.7 5.5 copy.96
  1077.2 8.2 convolution_bitcast_fusion
  1085.4 10.7 copy.72
  1096.1 5.4 all-to-all-start.1
  1102.1 201.2 %all-to-all-done.1 = f32[16,1,16,1,128,128]{5,4,2,3,1,0:T(8,128)} async-done(((f32[16,1,16,1,128,128]{5,4,2,3,1,0:T(8,128)}), f32[16,1,16,1,128,128]{5,4,2,3,1,0:T(8,128)}, u32[]{:S(2)}, u32[]{:S(2)}) %all-to-all-start.1) | async-done | bytes 16777248 | tf_op jit(solution)/shard_map/all_to_all | solution.py:102
  1303.2 32.3 %fusion.5 = f32[2,16,128,6,128]{4,3,2,1,0:T(8,128)} fusion(f32[2,8,16,128,128]{4,3,2,1,0:T(8,128)} %bitcast.15, f32[2,8,6]{1,2,0:T(8,128)S(1)} %convert_reduce_fusion), kind=kOutput, calls=%fused_computation.8 | convolution fusion | flops 301989888 | bytes 29360512 | tf_op jit(solution)/shard_map/cqus,cqupryz->cprysz/dot_general | solution.py:109
  1335.5 17.1 fusion.12
  1355.8 101.7 %all-gather.13.cloned.1.call-done = f32[4096,256]{1,0:T(8,128)} async-done(((f32[256,256]{1,0:T(8,128)}), f32[4096,256]{1,0:T(8,128)}) %all-gather.13.cloned.1.call-update) | async-done | bytes 4194320 | tf_op jit(solution)/shard_map/all_gather | solution.py:12
  1457.6 2.5 reduce_sum.77
  1460.2 11.7 cholesky.49
  1472.0 9.8 custom-call.14
  1482.3 11.7 cholesky.103
  1496.9 4.3 while.1
  1501.2 19.7 %custom-call.15 = f32[2,128,128]{1,2,0:T(8,128)S(1)} custom-call(f32[2,128,128]{2,1,0:T(8,128)S(1)} %get-tuple-element.12), custom_call_target="InvertDiagBlocksLowerTriangular" | custom-call | tf_op jit(solution)/shard_map/triangular_solve | solution.py:21
  1523.6 2.1 fusion.28
  1525.8 71.1 %all-gather.15.cloned.1.call-done = f32[12288,256]{1,0:T(8,128)} async-done(((f32[768,256]{1,0:T(8,128)}), f32[12288,256]{1,0:T(8,128)}) %all-gather.15.cloned.1.call-update) | async-done | bytes 12582928 | tf_op jit(solution)/shard_map/all_gather | solution.py:12
  1596.9 5.5 reduce_sum.78
  1603.4 179.4 %all-gather.17.cloned.1.call-done = f32[12288,256]{1,0:T(8,128)} async-done(((f32[768,256]{1,0:T(8,128)}), f32[12288,256]{1,0:T(8,128)}) %all-gather.17.cloned.1.call-update) | async-done | bytes 12582928 | tf_op jit(solution)/shard_map/all_gather | solution.py:12
  1782.8 6.4 reduce_sum.79
  1789.2 3.5 select_subtract_fusion
  (81 shorter events, 23.6 us)
Async XLA Ops:
  6.5 419.9 %all-gather.9.cloned.1.call-start = ((), (), s32[]{:S(2)}) async-start(), calls=%async_computation.2 | async-start | bytes 35651584 | tf_op jit(solution)/shard_map/all_gather | solution.py:12
  10.9 0.8 copy-start.3
  10.9 827.6 %all-gather.11.cloned.1.call-start = ((), (), s32[]{:S(2)}) async-start(), calls=%async_computation.3 | async-start | bytes 35651584 | tf_op jit(solution)/shard_map/all_gather | solution.py:12
  16.2 423.9 %copy-start = (f32[1,512,1024]{2,1,0:T(8,128)S(1)}, f32[1,512,1024]{2,1,0:T(8,128)}, u32[]{:S(2)}) copy-start(f32[1,512,1024]{2,1,0:T(8,128)} %param.5) | copy-start | bytes 6291460
  851.9 5.2 copy-start.1
  874.6 197.1 %all-to-all-start = ((f32[16,1,128,1024]{3,2,1,0:T(8,128)}), f32[16,1,128,1024]{3,2,1,0:T(8,128)}, u32[]{:S(2)}, u32[]{:S(2)}) async-start(f32[16,1,128,1024]{3,2,1,0:T(8,128)} %copy.71), calls=%async_computation | async-start | bytes 16777216 | tf_op jit(solution)/shard_map/all_to_all | solution.py:99
  1096.1 207.2 %all-to-all-start.1 = ((f32[16,1,16,1,128,128]{5,4,2,3,1,0:T(8,128)}), f32[16,1,16,1,128,128]{5,4,2,3,1,0:T(8,128)}, u32[]{:S(2)}, u32[]{:S(2)}) async-start(f32[16,1,16,1,128,128]{5,4,2,3,1,0:T(8,128)} %copy.72), calls=%async_computation.1 | async-start | bytes 33554432 | tf_op jit(solution)/shard_map/all_to_all | solution.py:102
  1101.5 356.1 %all-gather.13.cloned.1.call-start = ((), (), s32[]{:S(2)}) async-start(), calls=%async_computation.4 | async-start | bytes 4456448 | tf_op jit(solution)/shard_map/all_gather | solution.py:12
  1352.6 1.7 copy-start.2
  1355.7 241.1 %all-gather.15.cloned.1.call-start = ((), (), s32[]{:S(2)}) async-start(), calls=%async_computation.5 | async-start | bytes 13369344 | tf_op jit(solution)/shard_map/all_gather | solution.py:12
  1525.8 257.0 %all-gather.17.cloned.1.call-start = ((), (), s32[]{:S(2)}) async-start(), calls=%async_computation.6 | async-start | bytes 13369344 | tf_op jit(solution)/shard_map/all_gather | solution.py:12
Sparse Core Ops, SparseCore 0:
  11.0 415.4 all-gather.8
  429.1 409.3 all-gather.10
  1355.9 101.6 all-gather.12
  1525.9 70.9 all-gather.14
  1603.4 179.3 all-gather.16
